TPU v7x, 32 devices: a whole 2x2x4 slice. The times are simulated.
32 devices in a mesh: groups: 2 (over x), mp: 16 (over z, y, core).
Axes of the slice: x: 2, y: 2, z: 4, core: 2. Of those that a mesh axis runs over, the one named last changes fastest.
Arguments:
- hidden_in: bfloat16 [1536, 2560], P(('groups', 'mp')), parts along dimension 0, may hold values from -6 to 6
- ln_gain: float32 [2560], replicated, may hold values from 0.1 to 1.9
- w_qkv: bfloat16 [3, 2560, 2048], P(None, None, 'mp'), may hold values from -2 to 2
- w_out: bfloat16 [2048, 2560], P('mp'), may hold values from -0.125 to 0.125
- residue_index: int32 [1536], P('groups'), parts along dimension 0, may hold values from 0 to 1343, as said below
- w_map: bfloat16 [32, 128], replicated, may hold values from -1 to 1, as said below
- relpos_table: float32 [65, 128], replicated, may hold values from -0.75 to 0.75
- w_side: bfloat16 [2, 2560, 128], replicated, may hold values from -0.009765625 to 0.009765625
- tri_gain: float32 [2, 128], replicated, may hold values from 0.1 to 1.9
- w_tri: bfloat16 [5, 128, 128], replicated, may hold values from -0.5 to 0.5
- w_tri_out: bfloat16 [128, 128], replicated, may hold values from -0.5 to 0.5
Outputs:
- hidden_out: bfloat16 [1536, 2560], P(('groups', 'mp')), parts along dimension 0
- pair_out: bfloat16 [1536, 768, 128], P(('groups', 'mp')), parts along dimension 0
There are 2 independent parts, one for each index of `groups`. A program takes and returns all parts, laid end to end along the dimension named above; an argument that names none is the same for every part. Nothing has to cross between parts.
Inputs may be any that keep to these rules, and one draw needn't show every extreme that they name: `w_map`: each column sums to zero over the 32 heads before rounding to bfloat16. `residue_index`: strictly increasing from 0; consecutive entries differ by 1 or by 25, exactly 24 of them by 25.
All inputs are finite; a program needn't handle non-finite values.
Results may differ from a plain program's by a relative error of at most 0.011.
Values may be sent and summed in bfloat16 or wider, within the bound.
A program may use at most 192 MiB of HBM per device.

v0:
```python
import jax
import jax.numpy as jnp
from jax import lax
from jax.sharding import PartitionSpec as P

HD = 64
BINS = 65


def layer_norm(tensor, gain_vec, norm_axis):
    center = jnp.mean(tensor, axis=norm_axis, keepdims=True)
    centered = tensor - center
    variance = jnp.mean(centered * centered, axis=norm_axis, keepdims=True)
    return centered * lax.rsqrt(variance + 1e-05) * gain_vec


def rotary_tables(length, width):
    inv_freq = 1.0 / 10000.0 ** (jnp.arange(0, width, 2, dtype=jnp.float32) / width)
    angles = jnp.arange(length, dtype=jnp.float32)[:, None] * inv_freq[None, :]
    angles = jnp.concatenate([angles, angles], axis=-1)
    return (jnp.cos(angles)[:, None, :], jnp.sin(angles)[:, None, :])


def rotate(tensor, cos_table, sin_table):
    middle = tensor.shape[-1] // 2
    turned = jnp.concatenate([-tensor[..., middle:], tensor[..., :middle]], axis=-1)
    return tensor * cos_table + turned * sin_table


def per_device(
    hidden_in,
    ln_gain,
    w_qkv,
    w_out,
    residue_index,
    w_map,
    relpos_table,
    w_side,
    tri_gain,
    w_tri,
    w_tri_out,
):
    local_rows = hidden_in.shape[0]
    devices_mp = lax.axis_size("mp")
    length = local_rows * devices_mp
    local_heads = w_qkv.shape[2] // HD
    normed = layer_norm(hidden_in.astype(jnp.float32), ln_gain, -1).astype(jnp.bfloat16)
    projected = jnp.einsum(
        "rd,tdh->trh",
        lax.all_gather(normed, "mp", axis=0, tiled=True),
        w_qkv,
        preferred_element_type=jnp.float32,
    )
    projected = projected.reshape(3, length, local_heads, HD)
    cos_table, sin_table = rotary_tables(length, HD)
    queries = rotate(projected[0] * HD ** (-0.5), cos_table, sin_table).astype(jnp.bfloat16)
    key_rows = rotate(projected[1], cos_table, sin_table).astype(jnp.bfloat16)
    value_rows = projected[2].astype(jnp.bfloat16)
    scores = jnp.einsum("qhd,khd->hqk", queries, key_rows, preferred_element_type=jnp.float32)
    attn_probs = jax.nn.softmax(scores, axis=-1).astype(jnp.bfloat16)
    attended = jnp.einsum(
        "hqk,khd->qhd", attn_probs, value_rows, preferred_element_type=jnp.float32
    )
    attended = attended.astype(jnp.bfloat16).reshape(length, local_heads * HD)
    mixed = lax.psum_scatter(
        jnp.dot(attended, w_out, preferred_element_type=jnp.float32).astype(jnp.bfloat16),
        "mp",
        scatter_dimension=0,
        tiled=True,
    ).astype(jnp.float32)
    hidden_out = (hidden_in.astype(jnp.float32) + mixed).astype(jnp.bfloat16)
    attn_maps = lax.all_to_all(attn_probs, "mp", split_axis=1, concat_axis=0, tiled=True)
    pair_sum = length * jnp.einsum(
        "hij,hc->ijc", attn_maps, w_map, preferred_element_type=jnp.float32
    )
    row_start = lax.axis_index("mp") * local_rows
    row_index = lax.dynamic_slice_in_dim(residue_index, row_start, local_rows, 0)
    reach = (BINS - 1) // 2
    rel_bins = jnp.clip(residue_index[None, :] - row_index[:, None], -reach, reach) + reach
    one_hot = (rel_bins[None, :, :] == jnp.arange(BINS, dtype=jnp.int32)[:, None, None]).astype(
        jnp.float32
    )
    pair_sum = pair_sum + jnp.einsum(
        "nij,nc->ijc", one_hot, relpos_table, precision=lax.Precision.HIGHEST
    )
    side_terms = jnp.einsum(
        "rd,sdc->src", hidden_out, w_side, preferred_element_type=jnp.float32
    ).astype(jnp.bfloat16)
    right_rows = lax.all_gather(side_terms[1], "mp", axis=0, tiled=True)
    pair_sum = (
        pair_sum
        + side_terms[0][:, None, :].astype(jnp.float32)
        + right_rows[None, :, :].astype(jnp.float32)
    )
    pair_normed = layer_norm(pair_sum, tri_gain[0], -1).astype(jnp.bfloat16)
    edges = jnp.einsum("ijc,pcd->pdij", pair_normed, w_tri[:4], preferred_element_type=jnp.float32)
    left_edge = (jax.nn.sigmoid(edges[1]) * edges[0]).astype(jnp.bfloat16)
    right_edge = (jax.nn.sigmoid(edges[3]) * edges[2]).astype(jnp.bfloat16)
    out_gate = jax.nn.sigmoid(
        jnp.einsum("ijc,cd->ijd", pair_normed, w_tri[4], preferred_element_type=jnp.float32)
    )
    channels = left_edge.shape[0]
    group = channels // devices_mp
    shape_four = (devices_mp, group, local_rows, length)
    lefts = lax.all_to_all(
        left_edge.reshape(shape_four), "mp", split_axis=0, concat_axis=2, tiled=True
    )
    rights = lax.all_to_all(
        right_edge.reshape(shape_four), "mp", split_axis=0, concat_axis=2, tiled=True
    )
    products = jnp.einsum(
        "xcik,xcjk->xcij", lefts, rights, preferred_element_type=jnp.float32
    ).astype(jnp.bfloat16)
    returned = lax.all_to_all(products, "mp", split_axis=2, concat_axis=0, tiled=True).reshape(
        channels, local_rows, length
    )
    prod_normed = layer_norm(returned.astype(jnp.float32), tri_gain[1][:, None, None], 0).astype(
        jnp.bfloat16
    )
    projected_out = jnp.einsum(
        "cij,cd->ijd", prod_normed, w_tri_out, preferred_element_type=jnp.float32
    )
    pair_out = (pair_sum + out_gate * projected_out).astype(jnp.bfloat16)
    return (hidden_out, pair_out)


def solution(mesh):
    placed = (
        P(("groups", "mp"), None),
        P(),
        P(None, None, "mp"),
        P("mp", None),
        P("groups"),
        P(),
        P(),
        P(),
        P(),
        P(),
        P(),
    )
    return jax.shard_map(
        per_device,
        mesh=mesh,
        in_specs=placed,
        out_specs=(P(("groups", "mp"), None), P(("groups", "mp"), None, None)),
        check_vma=False,
    )
```

profile of v0, /device:TPU:0, one launch (start us, length us, event | category | flops | bytes accessed | tf_op | source)
XLA Modules:
  0.0 1073.3 jit_solution(85845607730882438)
XLA Ops:
  7.2 1.2 convert_reduce_fusion
  8.4 1.2 fusion.25
  9.6 1.8 fusion.27
  11.5 2.7 copy.59
  14.3 1.1 fusion.35
  15.4 48.0 %all-gather.3.cloned.1.call-done = bf16[768,2560]{1,0:T(8,128)(2,1)} async-done(((bf16[48,2560]{1,0:T(8,128)(2,1)}), bf16[768,2560]{1,0:T(8,128)(2,1)}) %all-gather.3.cloned.1.call-update) | async-done | bytes 3932176 | tf_op jit(solution)/shard_map/all_gather | solution.py:50
  63.4 3.9 fusion.48
  67.6 3.5 fusion.46
  71.1 2.7 divide_convert_fusion
  73.9 1.4 copy-done.2
  75.3 0.5 convolution_convert_fusion.1
  75.8 3.1 convolution_convert_fusion
  79.0 6.9 copy.61
  85.9 5.1 all-to-all-start
  91.1 0.5 slice_bitcast_fusion.1
  91.7 60.6 %all-to-all-done = bf16[2,768,768]{2,0,1:T(2,128)(2,1)} async-done(((bf16[2,768,768]{2,0,1:T(2,128)(2,1)}), bf16[2,768,768]{2,0,1:T(2,128)(2,1)}, u32[]{:S(2)}, u32[]{:S(2)}) %all-to-all-start) | async-done | bytes 2359328 | tf_op jit(solution)/shard_map/all_to_all | solution.py:72
  152.3 2.0 copy.62
  154.3 3.8 copy.63
  158.1 6.1 all_to_all.45
  164.2 10.8 %fusion.43 = f32[48,768,128]{1,2,0:T(8,128)} fusion(bf16[32,48,768]{2,0,1:T(8,128)(2,1)} %all_to_all.45, bf16[32,128]{1,0:T(8,128)(2,1)S(1)} %copy-done.11), kind=kOutput, calls=%fused_computation.80 | convolution fusion | flops 301989888 | bytes 21241856 | tf_op jit(solution)/shard_map/hij,hc->ijc/dot_general | solution.py:73
  175.1 1.0 fusion.28
  176.1 0.3 fusion.20
  176.5 32.5 %all-gather = bf16[1,768,128]{2,1,0:T(8,128)(2,1)S(1)} all-gather(bf16[1,48,128]{2,1,0:T(8,128)(2,1)S(1)} %get-tuple-element.24), channel_id=2, replica_groups=mesh['groups'=2,'mp'=16] {'mp'}, dimensions={1}, use_global_device_ids=true | all-gather | bytes 208896 | tf_op jit(solution)/shard_map/all_gather | solution.py:89
  209.0 0.2 copy.64
  209.2 18.6 %fusion.47 = (f32[48,768]{1,0:T(8,128)S(1)}, f32[48,768,128]{1,2,0:T(8,128)}) fusion(f32[768,128]{0,1:T(8,128)S(1)} %copy.64, f32[48,128]{1,0:T(8,128)S(1)} %get-tuple-element.23, f32[65,128]{1,0:T(8,128)S(1)} %copy-done.9, s32[48,768]{1,0:T(8,128)S(1)} %clamp_add_fusion, f32[48,768,128]{1,2,0:T(8,128)} %fusion.43), kind=kOutput, calls=%fused_computation.89 | convolution fusion | flops 3706454016 | bytes 38494720 | tf_op jit(solution)/shard_map/nij,nc->ijc/dot_general | solution.py:83
  227.8 9.5 multiply_reduce_fusion.1
  237.4 32.3 %convolution_bitcast_fusion = f32[4,128,48,768]{3,1,0,2:T(8,128)} fusion(bf16[5,128,128]{2,1,0:T(8,128)(2,1)S(1)} %copy-done.8, f32[48,768,128]{1,2,0:T(8,128)} %get-tuple-element.30, f32[128]{0:T(128)S(1)} %get-tuple-element.26, f32[48,768]{1,0:T(8,128)S(1)} %add_rsqrt_fusion.1, f32[48,768]{1,0:T(8,128)S(1)} %broadcast_multiply_fusion.3), kind=kOutput, calls=%fused_computation.1 | convolution fusion | flops 4850712576 | bytes 94798336 | tf_op jit(solution)/shard_map/ijc,pcd->pdij/dot_general | solution.py:96
  269.7 32.2 %fusion.18 = (bf16[16,8,48,768]{3,1,0,2:T(8,128)(2,1)}, bf16[16,8,48,768]{3,1,0,2:T(8,128)(2,1)}) fusion(f32[4,128,48,768]{3,1,0,2:T(8,128)} %convolution_bitcast_fusion), kind=kLoop, calls=%fused_computation.32 | loop fusion | flops 47185920 | bytes 94371840 | tf_op jit(solution)/shard_map/convert_element_type | solution.py:98
  301.9 8.3 copy.71
  310.2 4.8 all-to-all-start.2
  315.0 8.4 copy.69
  323.4 160.4 %all-to-all-done.2 = bf16[16,8,48,768]{3,1,2,0:T(8,128)(2,1)} async-done(((bf16[16,8,48,768]{3,1,2,0:T(8,128)(2,1)}), bf16[16,8,48,768]{3,1,2,0:T(8,128)(2,1)}, u32[]{:S(2)}, u32[]{:S(2)}) %all-to-all-start.2) | async-done | bytes 9437216 | tf_op jit(solution)/shard_map/all_to_all | solution.py:108
  483.8 40.7 %all-to-all-start.1 = ((bf16[16,8,48,768]{3,1,2,0:T(8,128)(2,1)}), bf16[16,8,48,768]{3,1,2,0:T(8,128)(2,1)}, u32[]{:S(2)}, u32[]{:S(2)}) async-start(bf16[16,8,48,768]{3,1,2,0:T(8,128)(2,1)} %copy.69), calls=%async_computation.2 | async-start | bytes 18874368 | tf_op jit(solution)/shard_map/all_to_all | solution.py:105
  524.5 9.2 copy.72
  533.8 159.6 %all-to-all-done.1 = bf16[16,8,48,768]{3,1,2,0:T(8,128)(2,1)} async-done(((bf16[16,8,48,768]{3,1,2,0:T(8,128)(2,1)}), bf16[16,8,48,768]{3,1,2,0:T(8,128)(2,1)}, u32[]{:S(2)}, u32[]{:S(2)}) %all-to-all-start.1) | async-done | bytes 9437216 | tf_op jit(solution)/shard_map/all_to_all | solution.py:105
  693.4 9.4 copy.70
  702.7 15.1 %convert_bitcast_fusion.1 = bf16[1,8,768,768]{3,2,1,0:T(8,128)(2,1)} fusion(bf16[8,768,768]{2,1,0:T(8,128)(2,1)} %bitcast.106, bf16[8,768,768]{2,1,0:T(8,128)(2,1)} %bitcast.105), kind=kOutput, calls=%fused_computation.30 | convolution fusion | flops 7252475904 | bytes 28311552 | tf_op jit(solution)/shard_map/xcik,xcjk->xcij/dot_general | solution.py:111
  717.8 12.7 %copy.73 = bf16[1,8,768,768]{3,1,0,2:T(8,128)(2,1)} copy(bf16[1,8,768,768]{3,2,1,0:T(8,128)(2,1)} %convert_bitcast_fusion.1) | data formatting | bytes 18874368 | tf_op jit(solution)/shard_map/convert_element_type | solution.py:113
  730.5 245.4 %all_to_all.57 = bf16[1,8,768,768]{3,1,0,2:T(8,128)(2,1)} all-to-all(bf16[1,8,768,768]{3,1,0,2:T(8,128)(2,1)} %copy.73), channel_id=1, replica_groups=mesh['groups'=2,'mp'=16] {'mp'}, dimensions={2} | all-to-all | bytes 18874368 | tf_op jit(solution)/shard_map/all_to_all | solution.py:114
  975.9 9.3 copy.74
  985.2 5.0 fusion.13
  990.2 12.8 %convert_bitcast_fusion = f32[16,1,8,48,768]{4,3,0,2,1:T(8,128)} fusion(bf16[1,8,16,48,768]{4,3,2,1,0:T(8,128)(2,1)} %bitcast.103), kind=kLoop, calls=%fused_computation.14 | loop fusion | flops 4718592 | bytes 28311552 | tf_op jit(solution)/shard_map/convert_element_type | solution.py:117
  1003.0 6.2 multiply_reduce_fusion
  1009.2 7.3 copy.75
  1016.6 4.1 fusion.11
  1020.7 8.4 fusion.15
  1029.1 24.5 %add_convert_fusion = bf16[48,768,128]{1,2,0:T(8,128)(2,1)} fusion(f32[48,768,128]{1,2,0:T(8,128)} %get-tuple-element.30, f32[48,768,128]{1,2,0:T(8,128)} %fusion.15, bf16[5,128,128]{2,1,0:T(8,128)(2,1)S(1)} %copy-done.8, f32[128]{0:T(128)S(1)} %get-tuple-element.26, f32[48,768]{1,0:T(8,128)S(1)} %add_rsqrt_fusion.1, f32[48,768]{1,0:T(8,128)S(1)} %broadcast_multiply_fusion.3), kind=kOutput, calls=%fused_computation.19 | convolution fusion | flops 1255145472 | bytes 66388480 | tf_op jit(solution)/shard_map/ijc,cd->ijd/dot_general | solution.py:100
  1053.7 12.6 %copy.78 = bf16[48,768,128]{2,1,0:T(8,128)(2,1)} copy(bf16[48,768,128]{1,2,0:T(8,128)(2,1)} %add_convert_fusion) | data formatting | bytes 18874368
  (51 shorter events, 0.9 us)
Async XLA Ops:
  7.2 168.9 %copy-start = (bf16[2,2560,128]{2,1,0:T(8,128)(2,1)S(1)}, bf16[2,2560,128]{2,1,0:T(8,128)(2,1)}, u32[]{:S(2)}) copy-start(bf16[2,2560,128]{2,1,0:T(8,128)(2,1)} %param.18) | copy-start | bytes 3932164
  7.2 56.2 %all-gather.3.cloned.1.call-start = ((), (), s32[]{:S(2)}) async-start(), calls=%async_computation.5 | async-start | bytes 4177920 | tf_op jit(solution)/shard_map/all_gather | solution.py:50
  11.4 163.6 %reduce-scatter.2.cloned.1.call-start = ((), (), s32[]{:S(2)}) async-start(), calls=%async_computation.6 | async-start | bytes 4177920 | tf_op jit(solution)/shard_map/reduce_scatter | solution.py:65
  63.4 4.1 copy-start.5
  63.4 4.1 copy-start.6
  67.4 8.4 copy-start.7
  73.9 1.4 copy-start.2
  75.8 15.2 %copy-start.12 = (s32[768]{0:T(1024)S(1)}, s32[768]{0:T(1024)}, u32[]{:S(2)}) copy-start(s32[768]{0:T(1024)} %param.15) | copy-start | bytes 9220
  75.8 15.3 %copy-start.14 = (f32[2,128]{1,0:T(2,128)S(1)}, f32[2,128]{1,0:T(2,128)}, u32[]{:S(2)}) copy-start(f32[2,128]{1,0:T(2,128)} %param.19) | copy-start | bytes 3076
  85.9 78.4 %copy-start.11 = (bf16[32,128]{1,0:T(8,128)(2,1)S(1)}, bf16[32,128]{1,0:T(8,128)(2,1)}, u32[]{:S(2)}) copy-start(bf16[32,128]{1,0:T(8,128)(2,1)} %param.16) | copy-start | bytes 24580
  85.9 66.5 %all-to-all-start = ((bf16[2,768,768]{2,0,1:T(2,128)(2,1)}), bf16[2,768,768]{2,0,1:T(2,128)(2,1)}, u32[]{:S(2)}, u32[]{:S(2)}) async-start(bf16[2,768,768]{2,0,1:T(2,128)(2,1)} %copy.61), calls=%async_computation.1 | async-start | bytes 4718592 | tf_op jit(solution)/shard_map/all_to_all | solution.py:72
  164.2 10.8 %copy-start.3 = (bf16[48,2560]{1,0:T(8,128)(2,1)S(1)}, bf16[48,2560]{1,0:T(8,128)(2,1)}, u32[]{:S(2)}) copy-start(bf16[48,2560]{1,0:T(8,128)(2,1)} %param.11) | copy-start | bytes 737284
  164.2 44.9 %copy-start.9 = (f32[65,128]{1,0:T(8,128)S(1)}, f32[65,128]{1,0:T(8,128)}, u32[]{:S(2)}) copy-start(f32[65,128]{1,0:T(8,128)} %param.17) | copy-start | bytes 99844
  176.1 32.9 %copy-start.4 = (bf16[48,2560]{1,0:T(8,128)(2,1)}, bf16[48,2560]{1,0:T(8,128)(2,1)S(1)}, u32[]{:S(2)}) copy-start(bf16[48,2560]{1,0:T(8,128)(2,1)S(1)} %fusion.28) | copy-start | bytes 737284
  227.8 9.6 copy-start.8
  310.2 173.6 %all-to-all-start.2 = ((bf16[16,8,48,768]{3,1,2,0:T(8,128)(2,1)}), bf16[16,8,48,768]{3,1,2,0:T(8,128)(2,1)}, u32[]{:S(2)}, u32[]{:S(2)}) async-start(bf16[16,8,48,768]{3,1,2,0:T(8,128)(2,1)} %copy.71), calls=%async_computation.3 | async-start | bytes 18874368 | tf_op jit(solution)/shard_map/all_to_all | solution.py:108
  483.8 209.6 %all-to-all-start.1 = ((bf16[16,8,48,768]{3,1,2,0:T(8,128)(2,1)}), bf16[16,8,48,768]{3,1,2,0:T(8,128)(2,1)}, u32[]{:S(2)}, u32[]{:S(2)}) async-start(bf16[16,8,48,768]{3,1,2,0:T(8,128)(2,1)} %copy.69), calls=%async_computation.2 | async-start | bytes 18874368 | tf_op jit(solution)/shard_map/all_to_all | solution.py:105
  1009.2 7.3 copy-start.13
  1016.6 4.1 copy-start.10
  1029.1 37.1 %copy-start.1 = (bf16[2,2560,128]{2,1,0:T(8,128)(2,1)S(1)}, bf16[2,2560,128]{2,1,0:T(8,128)(2,1)}, u32[]{:S(2)}) copy-start(bf16[2,2560,128]{2,1,0:T(8,128)(2,1)} %param.18) | copy-start | bytes 3932164
Sparse Core Ops, SparseCore 0:
  11.5 51.7 all-gather.2
  79.1 91.6 reduce-scatter.1
where the time goes:
time: 1080 us; the launch traced here: 1070 us
  waiting for transfers between devices  429 us (40%)
  blocking collectives  278 us (26%)
  matrix products  121 us (11%)
  local copies, waits for them, and re-layouts  101 us (9%)
  other arithmetic  79.3 us (7%)
  starting transfers between devices  50.7 us (5%)
  between operations  14.6 us (1%)
    all_to_all x1, blocking collectives, per_device(): lax.all_to_all(products, 'mp', split_axis=2, concat_axis=0, tiled=True)  245 us
    all_to_all x1, waiting for transfers between devices, per_device(): lax.all_to_all(right_edge.reshape(shape_four), 'mp', split_axis=0, concat...  160 us
    all_to_all x1, waiting for transfers between devices, per_device(): lax.all_to_all(left_edge.reshape(shape_four), 'mp', split_axis=0, concat_...  160 us
    all_to_all x1, waiting for transfers between devices, per_device(): lax.all_to_all(attn_probs, 'mp', split_axis=1, concat_axis=0, tiled=True)  60.6 us
    all_gather x1, waiting for transfers between devices, per_device(): lax.all_gather(normed, 'mp', axis=0, tiled=True)  48 us
    all_to_all x1, starting transfers between devices, per_device(): lax.all_to_all(left_edge.reshape(shape_four), 'mp', split_axis=0, concat_...  40.7 us
    all_gather x1, blocking collectives, per_device(): right_rows = lax.all_gather(side_terms[1], 'mp', axis=0, tiled=True)  32.5 us
    dot_general x1, matrix products, per_device(): jnp.einsum('ijc,pcd->pdij', pair_normed, w_tri[:4], preferred_element_typ...  32.3 us
  transfers between devices with their start and end apart: 5, of which 4 were waited for; matrix products, arithmetic and copies ran while one was open for 4% of the time, Pallas kernels for 0%

commit v1 on v0

v1 whole, which is shorter than its diff:
```python
import functools

import jax
import jax.numpy as jnp
from jax import lax
from jax.experimental import pallas as pl
from jax.experimental.pallas import tpu as pltpu
from jax.sharding import PartitionSpec as P

HD = 64
BINS = 65
BIN_ROWS = 80
LANES = 128
CHUNKS = 3
VMEM_BYTES = 60 * 1024 * 1024


def layer_norm(tensor, gain_vec, norm_axis):
    center = jnp.mean(tensor, axis=norm_axis, keepdims=True)
    centered = tensor - center
    variance = jnp.mean(centered * centered, axis=norm_axis, keepdims=True)
    return centered * lax.rsqrt(variance + 1e-05) * gain_vec


def rotary_tables(length, width):
    inv_freq = 1.0 / 10000.0 ** (jnp.arange(0, width, 2, dtype=jnp.float32) / width)
    angles = jnp.arange(length, dtype=jnp.float32)[:, None] * inv_freq[None, :]
    angles = jnp.concatenate([angles, angles], axis=-1)
    return (jnp.cos(angles)[:, None, :], jnp.sin(angles)[:, None, :])


def rotate(tensor, cos_table, sin_table):
    middle = tensor.shape[-1] // 2
    turned = jnp.concatenate([-tensor[..., middle:], tensor[..., :middle]], axis=-1)
    return tensor * cos_table + turned * sin_table


def two_terms(value):
    high = lax.reduce_precision(value, 8, 7)
    return high.astype(jnp.bfloat16), (value - high).astype(jnp.bfloat16)


def maps_kernel(q_ref, k_ref, out_ref, scratch):
    heads, rows, _ = q_ref.shape
    blocks = scratch.shape[0]

    def one_head(h, carry):
        scores = jnp.dot(q_ref[h], k_ref[h], preferred_element_type=jnp.float32)
        top = jnp.max(scores, axis=-1, keepdims=True)
        powers = jnp.exp(scores - top)
        probs = powers / jnp.sum(powers, axis=-1, keepdims=True)
        start = pl.multiple_of(h * rows, 8)
        for n in range(blocks):
            scratch[n, pl.ds(start, rows), :] = probs[:, n * LANES : (n + 1) * LANES]
        return carry

    lax.fori_loop(0, heads, one_head, 0, unroll=2)

    def one_row(j, carry):
        for n in range(blocks):
            rows_of = scratch[n, pl.ds(j, heads, stride=rows), :]
            out_ref[j, :, n * LANES : (n + 1) * LANES] = rows_of.astype(jnp.bfloat16)
        return carry

    lax.fori_loop(0, rows, one_row, 0, unroll=2)


def attention_maps(queries, keys, block):
    heads, rows, width = queries.shape
    length = keys.shape[2]
    return pl.pallas_call(
        maps_kernel,
        out_shape=jax.ShapeDtypeStruct((rows, heads, length), jnp.bfloat16),
        grid=(rows // block,),
        in_specs=[
            pl.BlockSpec((heads, block, width), lambda b: (0, b, 0)),
            pl.BlockSpec((heads, width, length), lambda b: (0, 0, 0)),
        ],
        out_specs=pl.BlockSpec((block, heads, length), lambda b: (b, 0, 0)),
        scratch_shapes=[pltpu.VMEM((length // LANES, heads * block, LANES), jnp.float32)],
        compiler_params=pltpu.CompilerParams(vmem_limit_bytes=VMEM_BYTES),
        cost_estimate=pl.CostEstimate(
            flops=2 * heads * rows * length * width * 4,
            bytes_accessed=2 * heads * rows * length,
            transcendentals=heads * rows * length,
        ),
        name="attention_maps",
    )(queries, keys)


def edges_kernel(own, row_index, maps_ref, mix_ref, right_ref, gain_ref, w_ref, cols_ref, *rest):
    scratch = rest[-1]
    block, heads, length = maps_ref.shape
    channels = right_ref.shape[0]
    width = gain_ref.shape[1]
    eye_rows = mix_ref.shape[2] - 2 * heads - 2 * BIN_ROWS
    reach = (BINS - 1) // 2
    first = pl.program_id(0) * block

    def one_row(j, carry):
        here = row_index[first + j]
        place = lax.broadcasted_iota(jnp.int32, (eye_rows, width), 0)
        eye = jnp.where(place == j, 1.0, 0.0).astype(jnp.bfloat16)
        for n in range(length // width):
            cols = slice(n * width, (n + 1) * width)
            bins = jnp.clip(cols_ref[:, cols] - here, -reach, reach) + reach
            places = lax.broadcasted_iota(jnp.int32, (BIN_ROWS, width), 0)
            hot = jnp.where(places == bins, 1.0, 0.0).astype(jnp.bfloat16)
            probs = maps_ref[j, :, cols]
            terms = jnp.concatenate([probs, probs, eye, hot, hot], axis=0)
            pair = jnp.dot(mix_ref[0], terms, preferred_element_type=jnp.float32)
            pair = pair + right_ref[:, cols]
            center = jnp.sum(pair, axis=0, keepdims=True) * (1.0 / channels)
            centered = pair - center
            variance = jnp.sum(centered * centered, axis=0, keepdims=True) * (1.0 / channels)
            normed = centered * lax.rsqrt(variance + 1e-05) * gain_ref[...]
            gated = jnp.dot(
                w_ref[...], normed.astype(jnp.bfloat16), preferred_element_type=jnp.float32
            )
            value = gated[:channels]
            edge = value + value * jnp.tanh(gated[channels : 2 * channels])
            start = pl.multiple_of(j * channels, 8)
            for m in range(width // LANES):
                scratch[n * (width // LANES) + m, pl.ds(start, channels), :] = edge[
                    :, m * LANES : (m + 1) * LANES
                ]
            if own:
                rest[2][j, :, cols] = pair
                rest[3][j, :, cols] = (0.5 + 0.5 * jnp.tanh(gated[2 * channels :])).astype(
                    jnp.bfloat16
                )
        return carry

    lax.fori_loop(0, block, one_row, 0)
    half = channels // 2

    def one_channel(c, carry):
        for n in range(length // LANES):
            for side in range(2):
                rows_of = scratch[n, pl.ds(c + side * half, block, stride=channels), :]
                rest[side][c, :, n * LANES : (n + 1) * LANES] = rows_of.astype(jnp.bfloat16)
        return carry

    lax.fori_loop(0, half, one_channel, 0, unroll=2)


def edges(own, row_index, maps, mix, right, gain, weights, cols, block, skip=0, rows=None):
    _, heads, length = maps.shape
    rows = maps.shape[0] if rows is None else rows
    channels = right.shape[0]
    half = channels // 2
    out_shape = [jax.ShapeDtypeStruct((half, rows, length), jnp.bfloat16)] * 2
    out_specs = [pl.BlockSpec((half, block, length), lambda b, s: (0, b, 0))] * 2
    if own:
        out_shape += [
            jax.ShapeDtypeStruct((rows, channels, length), jnp.float32),
            jax.ShapeDtypeStruct((rows, channels, length), jnp.bfloat16),
        ]
        out_specs += [pl.BlockSpec((block, channels, length), lambda b, s: (b, 0, 0))] * 2
    first = skip // block
    return pl.pallas_call(
        functools.partial(edges_kernel, own),
        out_shape=out_shape,
        grid_spec=pltpu.PrefetchScalarGridSpec(
            num_scalar_prefetch=1,
            grid=(rows // block,),
            in_specs=[
                pl.BlockSpec((block, heads, length), lambda b, s: (b + first, 0, 0)),
                pl.BlockSpec((1,) + mix.shape[1:], lambda b, s: (b, 0, 0)),
                pl.BlockSpec(right.shape, lambda b, s: (0, 0)),
                pl.BlockSpec(gain.shape, lambda b, s: (0, 0)),
                pl.BlockSpec(weights.shape, lambda b, s: (0, 0)),
                pl.BlockSpec(cols.shape, lambda b, s: (0, 0)),
            ],
            out_specs=out_specs,
            scratch_shapes=[pltpu.VMEM((length // LANES, block * channels, LANES), jnp.float32)],
        ),
        compiler_params=pltpu.CompilerParams(vmem_limit_bytes=VMEM_BYTES),
        cost_estimate=pl.CostEstimate(
            flops=2 * rows * length * channels * 800,
            bytes_accessed=2 * rows * length * channels,
            transcendentals=rows * length * channels,
        ),
        name="own_edges" if own else "right_edges",
    )(row_index, maps, mix, right, gain, weights, cols)


def final_kernel(core, mine_ref, theirs_ref, pair_ref, gate_ref, gain_ref, w_ref, out_ref, scratch):
    half, block, width = mine_ref.shape[1:]
    for n, ref in enumerate((mine_ref, theirs_ref)):

        def one_channel(c, carry):
            start = pl.multiple_of(c * block, 8)
            scratch[n, pl.ds(start, block), :] = ref[0, c].astype(jnp.float32)
            return carry

        lax.fori_loop(0, half, one_channel, 0, unroll=4)

    def one_row(i, carry):
        products = jnp.concatenate(
            [scratch[n, pl.ds(i, half, stride=block), :] for n in range(2)], axis=0
        )
        center = jnp.mean(products, axis=0, keepdims=True)
        centered = products - center
        variance = jnp.mean(centered * centered, axis=0, keepdims=True)
        normed = (centered * lax.rsqrt(variance + 1e-05) * gain_ref[...]).astype(jnp.bfloat16)
        projected = jnp.dot(w_ref[...], normed, preferred_element_type=jnp.float32)
        total = pair_ref[i] + gate_ref[i].astype(jnp.float32) * projected
        out_ref[i] = total.T.astype(jnp.bfloat16)
        return carry

    lax.fori_loop(0, block, one_row, 0, unroll=2)


def finish(core, mine, theirs, pair, gate, gain, weights, block):
    pieces, half, rows, width = mine.shape
    _, channels, length = pair.shape
    each = pieces // 2

    def column(u, core):
        side = u // each
        return (side + core[0] - 2 * side * core[0]) * each + u % each

    return pl.pallas_call(
        final_kernel,
        out_shape=jax.ShapeDtypeStruct((rows, length, channels), jnp.bfloat16),
        grid_spec=pltpu.PrefetchScalarGridSpec(
            num_scalar_prefetch=1,
            grid=(rows // block, pieces),
            in_specs=[
                pl.BlockSpec((1, half, block, width), lambda b, u, s: (u, 0, b, 0)),
                pl.BlockSpec(
                    (1, half, block, width), lambda b, u, s: ((u + each) % pieces, 0, b, 0)
                ),
                pl.BlockSpec((block, channels, width), lambda b, u, s: (b, 0, column(u, s))),
                pl.BlockSpec((block, channels, width), lambda b, u, s: (b, 0, column(u, s))),
                pl.BlockSpec(gain.shape, lambda b, u, s: (0, 0)),
                pl.BlockSpec(weights.shape, lambda b, u, s: (0, 0)),
            ],
            out_specs=pl.BlockSpec((block, width, channels), lambda b, u, s: (b, column(u, s), 0)),
            scratch_shapes=[pltpu.VMEM((2, half * block, width), jnp.float32)],
        ),
        compiler_params=pltpu.CompilerParams(vmem_limit_bytes=VMEM_BYTES),
        name="finish",
    )(core, mine, theirs, pair, gate, gain, weights)


def per_device(
    hidden_in,
    ln_gain,
    w_qkv,
    w_out,
    residue_index,
    w_map,
    relpos_table,
    w_side,
    tri_gain,
    w_tri,
    w_tri_out,
):
    local_rows = hidden_in.shape[0]
    devices_mp = lax.axis_size("mp")
    me = lax.axis_index("mp")
    core = lax.rem(me, 2)
    length = local_rows * devices_mp
    local_heads = w_qkv.shape[2] // HD
    heads, channels = w_map.shape
    swap = [(d, d ^ 1) for d in range(devices_mp)]
    normed = layer_norm(hidden_in.astype(jnp.float32), ln_gain, -1).astype(jnp.bfloat16)
    projected = jnp.einsum(
        "rd,tdh->trh",
        lax.all_gather(normed, "mp", axis=0, tiled=True),
        w_qkv,
        preferred_element_type=jnp.float32,
    )
    projected = projected.reshape(3, length, local_heads, HD)
    cos_table, sin_table = rotary_tables(length, HD)
    queries = rotate(projected[0] * HD ** (-0.5), cos_table, sin_table).astype(jnp.bfloat16)
    key_rows = rotate(projected[1], cos_table, sin_table).astype(jnp.bfloat16)
    value_rows = projected[2].astype(jnp.bfloat16)
    both = jnp.stack([queries.reshape(length, -1).T, key_rows.reshape(length, -1).T])
    gathered = lax.all_gather(both, "mp", axis=1, tiled=True)
    all_keys = gathered[1].reshape(heads, HD, length)
    all_queries = gathered[0].reshape(heads, HD, length).transpose(0, 2, 1)

    scores = jnp.einsum("qhd,khd->hqk", queries, key_rows, preferred_element_type=jnp.float32)
    attn_probs = jax.nn.softmax(scores, axis=-1).astype(jnp.bfloat16)
    attended = jnp.einsum(
        "hqk,khd->qhd", attn_probs, value_rows, preferred_element_type=jnp.float32
    )
    attended = attended.astype(jnp.bfloat16).reshape(length, local_heads * HD)
    mixed = lax.psum_scatter(
        jnp.dot(attended, w_out, preferred_element_type=jnp.float32).astype(jnp.bfloat16),
        "mp",
        scatter_dimension=0,
        tiled=True,
    ).astype(jnp.float32)
    hidden_out = (hidden_in.astype(jnp.float32) + mixed).astype(jnp.bfloat16)

    half_rows = length // 2
    row_start = me * local_rows
    half_start = core * half_rows
    own_maps = attention_maps(
        lax.dynamic_slice_in_dim(all_queries, row_start, local_rows, 1), all_keys, local_rows
    )
    map_block = 64 if half_rows % 64 == 0 else local_rows
    half_maps = attention_maps(
        lax.dynamic_slice_in_dim(all_queries, half_start, half_rows, 1), all_keys, map_block
    )

    side_terms = jnp.einsum(
        "rd,sdc->src", hidden_out, w_side, preferred_element_type=jnp.float32
    ).astype(jnp.bfloat16)
    all_sides = lax.all_gather(side_terms, "mp", axis=1, tiled=True)
    left_rows = all_sides[0]
    right = all_sides[1].astype(jnp.float32).T

    map_high, map_low = two_terms(w_map.astype(jnp.float32) * length)
    bin_high, bin_low = two_terms(relpos_table)
    bin_pad = ((0, BIN_ROWS - relpos_table.shape[0]), (0, 0))

    def mixing(left, block):
        count = left.shape[0] // block
        eye_rows = -(-block // 16) * 16
        lefts = jnp.pad(left.reshape(count, block, channels), ((0, 0), (0, eye_rows - block), (0, 0)))
        parts = [map_high, map_low, lefts, jnp.pad(bin_high, bin_pad), jnp.pad(bin_low, bin_pad)]
        parts = [jnp.broadcast_to(p, (count,) + p.shape[-2:]) for p in parts]
        return jnp.concatenate(parts, axis=1).transpose(0, 2, 1)

    turn = -core * (channels // 2)
    gain = jnp.broadcast_to(tri_gain[0][:, None], (channels, 2 * LANES))
    halved = w_tri * jnp.asarray(0.5, w_tri.dtype)
    right_w = jnp.concatenate([jnp.roll(halved[p].T, turn, axis=0) for p in (2, 3)], axis=0)
    left_w = jnp.concatenate(
        [jnp.roll(halved[p].T, turn, axis=0) for p in (0, 1)] + [halved[4].T], axis=0
    )
    cols = residue_index[None, :]

    block = 16 if local_rows % 16 == 0 else local_rows
    half_left = lax.dynamic_slice_in_dim(left_rows, half_start, half_rows, 0)
    half_index = lax.dynamic_slice_in_dim(residue_index, half_start, half_rows, 0)
    each = half_rows // CHUNKS
    kept, arriving = [], []
    r_block = 16 if each % 16 == 0 else each
    for n in range(CHUNKS):
        part = slice(n * each, (n + 1) * each)
        keep, send = edges(
            False,
            half_index[part],
            half_maps,
            mixing(half_left[part], r_block),
            right,
            gain,
            right_w,
            cols,
            r_block,
            n * each,
            each,
        )
        kept.append(keep)
        arriving.append(lax.ppermute(send, "mp", swap))
    left_keep, left_send, pair, gate = edges(
        True,
        lax.dynamic_slice_in_dim(residue_index, row_start, local_rows, 0),
        own_maps,
        mixing(lax.dynamic_slice_in_dim(left_rows, row_start, local_rows, 0), block),
        right,
        gain,
        left_w,
        cols,
        block,
    )
    lefts = jnp.concatenate([left_keep, lax.ppermute(left_send, "mp", swap)], axis=1)
    products = jnp.stack(
        [
            jnp.einsum("cik,cjk->cij", lefts, part, preferred_element_type=jnp.float32).astype(
                jnp.bfloat16
            )
            for part in kept + arriving
        ]
    )
    mine = products[:, :, :local_rows]
    theirs = lax.ppermute(products[:, :, local_rows:], "mp", swap)
    pair_out = finish(
        core[None],
        mine,
        theirs,
        pair,
        gate,
        jnp.broadcast_to(jnp.roll(tri_gain[1], turn)[:, None], (channels, each)),
        jnp.roll(w_tri_out, turn, axis=0).T,
        block,
    )
    return (hidden_out, pair_out)


def solution(mesh):
    placed = (
        P(("groups", "mp"), None),
        P(),
        P(None, None, "mp"),
        P("mp", None),
        P("groups"),
        P(),
        P(),
        P(),
        P(),
        P(),
        P(),
    )
    return jax.shard_map(
        per_device,
        mesh=mesh,
        in_specs=placed,
        out_specs=(P(("groups", "mp"), None), P(("groups", "mp"), None, None)),
        check_vma=False,
    )
```

time: 1080 us -> 901 us (0.83)
  Pallas kernels: 0 us -> 579 us
  waiting for transfers between devices: 429 us -> 155 us
  blocking collectives: 278 us -> 21.9 us
  other arithmetic: 79.3 us -> 12.4 us
  local copies, waits for them, and re-layouts: 101 us -> 42.3 us
  starting transfers between devices: 50.7 us -> 1.44 us
  matrix products: 121 us -> 74.1 us
    pallas_call x0 -> x7, Pallas kernels: none -> 579 us  [the longest x4 432 us: edges(): pl.pallas_call(functools.partial(edges_kernel, own), out_shape=out_shape,...]
    all_to_all x3 -> x0, waiting for transfers between devices: 381 us -> none  [the longest x1 160 us: per_device(): lax.all_to_all(right_edge.reshape(shape_four), 'mp', split_axis=0, concat...]
    all_to_all x1 -> x0, blocking collectives: 245 us -> none  [per_device(): lax.all_to_all(products, 'mp', split_axis=2, concat_axis=0, tiled=True)]
    reduce_scatter x1, waiting for transfers between devices: 0.01 us -> 62.2 us  [per_device(): lax.psum_scatter(jnp.dot(attended, w_out, preferred_element_type=jnp.floa...]
    dot_general x6, matrix products: 110 us -> 59 us  [per_device(): jnp.einsum('cik,cjk->cij', lefts, part, preferred_element_type=jnp.float32)]
    all_to_all x3 -> x0, starting transfers between devices: 50.6 us -> none  [the longest x1 40.7 us: per_device(): lax.all_to_all(left_edge.reshape(shape_four), 'mp', split_axis=0, concat_...]
    convert_element_type x6 -> x3, other arithmetic: 51.8 us -> 1.89 us  [the longest x1 1.11 us: per_device(): rotate(projected[0] * HD ** (-0.5), cos_table, sin_table)]
    convert_element_type x6 -> x3, local copies, waits for them, and re-layouts: 43.7 us -> 0.26 us  [the longest x2 0.24 us: two_terms(): return (high.astype(jnp.bfloat16), (value - high).astype(jnp.bfloat16))]
  transfers between devices with their start and end apart: 5 -> 8, of which waited for: 4 -> 5; matrix products, arithmetic and copies ran while one was open for 4% -> 9% of each run, Pallas kernels for 0% -> 36%
where the time goes in v1:
time: 901 us; the launch traced here: 900 us
  Pallas kernels  579 us (64%)
  waiting for transfers between devices  155 us (17%)
  matrix products  74.1 us (8%)
  local copies, waits for them, and re-layouts  42.3 us (5%)
  blocking collectives  21.9 us (2%)
  between operations  14.1 us (2%)
  other arithmetic  12.4 us (1%)
    pallas_call x4, Pallas kernels, edges(): pl.pallas_call(functools.partial(edges_kernel, own), out_shape=out_shape,...  432 us
    pallas_call x2, Pallas kernels, attention_maps(): pl.pallas_call(maps_kernel, out_shape=jax.ShapeDtypeStruct((rows, heads,...  89.1 us
    reduce_scatter x1, waiting for transfers between devices, per_device(): lax.psum_scatter(jnp.dot(attended, w_out, preferred_element_type=jnp.floa...  62.2 us
    dot_general x6, matrix products, per_device(): jnp.einsum('cik,cjk->cij', lefts, part, preferred_element_type=jnp.float32)  59 us
    pallas_call x1, Pallas kernels, finish(): pl.pallas_call(final_kernel, out_shape=jax.ShapeDtypeStruct((rows, length...  57.8 us
    all_gather x1, waiting for transfers between devices, per_device(): lax.all_gather(normed, 'mp', axis=0, tiled=True)  47.4 us
    all_gather x1, waiting for transfers between devices, per_device(): gathered = lax.all_gather(both, 'mp', axis=1, tiled=True)  33.5 us
    all_gather x1, blocking collectives, per_device(): all_sides = lax.all_gather(side_terms, 'mp', axis=1, tiled=True)  21.9 us
  transfers between devices with their start and end apart: 8, of which 5 were waited for; matrix products, arithmetic and copies ran while one was open for 9% of the time, Pallas kernels for 36%

profile of v1, /device:TPU:0, one launch (start us, length us, event | category | flops | bytes accessed | tf_op | source)
XLA Modules:
  0.0 900.5 jit_solution(2283102376884831607)
XLA Ops:
  7.2 1.2 convert_reduce_fusion
  8.4 1.2 fusion.8
  9.6 1.8 fusion.10
  11.5 4.0 copy.54
  15.9 47.4 %all-gather.3.cloned.1.call-done = bf16[768,2560]{1,0:T(8,128)(2,1)} async-done(((bf16[48,2560]{1,0:T(8,128)(2,1)}), bf16[768,2560]{1,0:T(8,128)(2,1)}) %all-gather.3.cloned.1.call-update) | async-done | bytes 3932176 | tf_op jit(solution)/shard_map/all_gather | solution.py:272
  63.4 4.4 fusion.36
  68.7 1.0 add_convert_fusion
  69.6 2.4 fusion.35
  72.0 3.6 fusion.2
  75.6 4.4 convolution_convert_fusion
  80.0 1.1 fusion.13
  81.1 0.8 pad_maximum_fusion
  82.7 0.8 fusion.21
  84.0 1.1 copy.65
  87.0 62.2 %reduce-scatter.2.cloned.1.call-done = bf16[48,2560]{1,0:T(8,128)(2,1)} async-done(((bf16[768,2560]{1,0:T(8,128)(2,1)}), bf16[48,2560]{1,0:T(8,128)(2,1)}) %reduce-scatter.2.cloned.1.call-update) | async-done | bytes 245776 | tf_op jit(solution)/shard_map/reduce_scatter | solution.py:292
  149.2 1.0 fusion.11
  150.9 21.9 %all_gather.11 = bf16[2,768,128]{2,0,1:T(2,128)(2,1)S(1)} all-gather(bf16[2,48,128]{2,0,1:T(2,128)(2,1)S(1)} %copy.59), channel_id=1, replica_groups=mesh['groups'=2,'mp'=16] {'mp'}, dimensions={1}, use_global_device_ids=true | all-gather | bytes 417792 | tf_op jit(solution)/shard_map/all_gather | solution.py:314
  174.5 1.3 concatenate.51
  175.8 1.3 concatenate.53
  177.3 1.3 concatenate.54
  178.6 0.8 convert_bitcast_fusion.right_ref
  179.4 33.5 %all-gather.5.cloned.1.call-done = bf16[2,2048,768]{2,1,0:T(8,128)(2,1)} async-done(((bf16[2,128,768]{2,1,0:T(8,128)(2,1)}), bf16[2,2048,768]{2,1,0:T(8,128)(2,1)}) %all-gather.5.cloned.1.call-update) | async-done | bytes 6291472 | tf_op jit(solution)/shard_map/all_gather | solution.py:282
  212.9 4.9 fusion.31
  217.8 1.6 copy-done.2
  219.7 3.0 copy.81
  222.6 77.5 %attention_maps.3.maps_ref = bf16[384,32,768]{2,1,0:T(8,128)(2,1)} custom-call(bf16[32,384,64]{2,1,0:T(8,128)(2,1)} %bitcast.123, bf16[32,64,768]{2,1,0:T(8,128)(2,1)} %bitcast.121), custom_call_target="tpu_custom_call" | custom-call | flops 4831838208 | bytes 18874368 | tf_op jit(solution)/shard_map/attention_maps/pallas_call | solution.py:71
  300.2 0.7 broadcast_in_dim.32.gain_ref
  300.9 123.2 %right_edges.3 = (bf16[64,128,768]{2,1,0:T(8,128)(2,1)}, bf16[64,128,768]{2,1,0:T(8,128)(2,1)}) custom-call(s32[128]{0:T(128)} %get-tuple-element.60.row_index, bf16[384,32,768]{2,1,0:T(8,128)(2,1)} %attention_maps.3.maps_ref, bf16[8,128,240]{2,1,0:T(8,128)(2,1)} %bitcast.140, f32[128,768]{1,0:T(8,128)} %convert_bitcast_fusion.right_ref, ...), custom_call_target="tpu_custom_call" | custom-call | flops 20132659200 | bytes 25165824 | tf_op jit(solution)/shard_map/right_edges/pallas_call | solution.py:161
  424.3 123.2 %right_edges.4 = (bf16[64,128,768]{2,1,0:T(8,128)(2,1)}, bf16[64,128,768]{2,1,0:T(8,128)(2,1)}) custom-call(s32[128]{0:T(128)} %get-tuple-element.59.row_index, bf16[384,32,768]{2,1,0:T(8,128)(2,1)} %attention_maps.3.maps_ref, bf16[8,128,240]{2,1,0:T(8,128)(2,1)} %bitcast.139, f32[128,768]{1,0:T(8,128)} %convert_bitcast_fusion.right_ref, ...), custom_call_target="tpu_custom_call" | custom-call | flops 20132659200 | bytes 25165824 | tf_op jit(solution)/shard_map/right_edges/pallas_call | solution.py:161
  547.8 123.2 %right_edges.5 = (bf16[64,128,768]{2,1,0:T(8,128)(2,1)}, bf16[64,128,768]{2,1,0:T(8,128)(2,1)}) custom-call(s32[128]{0:T(128)} %get-tuple-element.58.row_index, bf16[384,32,768]{2,1,0:T(8,128)(2,1)} %attention_maps.3.maps_ref, bf16[8,128,240]{2,1,0:T(8,128)(2,1)} %bitcast.138, f32[128,768]{1,0:T(8,128)} %convert_bitcast_fusion.right_ref, ...), custom_call_target="tpu_custom_call" | custom-call | flops 20132659200 | bytes 25165824 | tf_op jit(solution)/shard_map/right_edges/pallas_call | solution.py:161
  672.8 0.9 concatenate.48
  673.7 1.4 constant_dynamic-slice_fusion.5
  675.2 1.0 copy.77
  676.1 11.6 %attention_maps.2.maps_ref = bf16[48,32,768]{2,1,0:T(8,128)(2,1)} custom-call(bf16[32,48,64]{2,1,0:T(8,128)(2,1)} %bitcast.134, bf16[32,64,768]{2,1,0:T(8,128)(2,1)} %bitcast.122), custom_call_target="tpu_custom_call" | custom-call | flops 603979776 | bytes 2359296 | tf_op jit(solution)/shard_map/attention_maps/pallas_call | solution.py:71
  687.7 62.6 %own_edges.1 = (bf16[64,48,768]{2,1,0:T(8,128)(2,1)}, bf16[64,48,768]{2,1,0:T(8,128)(2,1)}, f32[48,128,768]{2,1,0:T(8,128)}, bf16[48,128,768]{2,1,0:T(8,128)(2,1)}) custom-call(s32[48]{0:T(128)} %dynamic_slice.25.row_index, bf16[48,32,768]{2,1,0:T(8,128)(2,1)} %attention_maps.2.maps_ref, bf16[3,128,240]{2,1,0:T(8,128)(2,1)} %bitcast.142, ...), custom_call_target="tpu_custom_call" | custom-call | flops 7549747200 | bytes 9437184 | tf_op jit(solution)/shard_map/own_edges/pallas_call | solution.py:161
  750.6 2.9 constant_dynamic-update-slice_fusion.1
  753.5 4.9 collective-permute-done
  759.1 9.8 %bitcast_dynamic-update-slice_fusion.5 = bf16[6,64,96,128]{3,2,1,0:T(8,128)(2,1)} fusion(bf16[64,96,768]{2,1,0:T(8,128)(2,1)S(1)} %constant_dynamic-update-slice_fusion, bf16[64,128,768]{2,1,0:T(8,128)(2,1)} %get-tuple-element.15), kind=kOutput, calls=%fused_computation.16 | convolution fusion | flops 1208745984 | bytes 23592960 | tf_op jit(solution)/shard_map/cik,cjk->cij/dot_general | solution.py:376
  768.9 9.8 %bitcast_dynamic-update-slice_fusion.4 = bf16[6,64,96,128]{3,2,1,0:T(8,128)(2,1)} fusion(bf16[6,64,96,128]{3,2,1,0:T(8,128)(2,1)} %bitcast_dynamic-update-slice_fusion.5, bf16[64,96,768]{2,1,0:T(8,128)(2,1)S(1)} %constant_dynamic-update-slice_fusion, bf16[64,128,768]{2,1,0:T(8,128)(2,1)} %get-tuple-element.16), kind=kOutput, calls=%fused_computation.15 | convolution fusion | flops 1208745984 | bytes 23592960 | tf_op jit(solution)/shard_map/cik,cjk->cij/dot_general | solution.py:376
  778.7 9.8 %bitcast_dynamic-update-slice_fusion.3 = bf16[6,64,96,128]{3,2,1,0:T(8,128)(2,1)} fusion(bf16[6,64,96,128]{3,2,1,0:T(8,128)(2,1)} %bitcast_dynamic-update-slice_fusion.4, bf16[64,96,768]{2,1,0:T(8,128)(2,1)S(1)} %constant_dynamic-update-slice_fusion, bf16[64,128,768]{2,1,0:T(8,128)(2,1)} %get-tuple-element.17), kind=kOutput, calls=%fused_computation.14 | convolution fusion | flops 1208745984 | bytes 23592960 | tf_op jit(solution)/shard_map/cik,cjk->cij/dot_general | solution.py:376
  788.5 9.8 %bitcast_dynamic-update-slice_fusion.2 = bf16[6,64,96,128]{3,2,1,0:T(8,128)(2,1)} fusion(bf16[6,64,96,128]{3,2,1,0:T(8,128)(2,1)} %bitcast_dynamic-update-slice_fusion.3, bf16[64,96,768]{2,1,0:T(8,128)(2,1)S(1)} %constant_dynamic-update-slice_fusion, bf16[64,128,768]{2,1,0:T(8,128)(2,1)} %collective-permute-done.1), kind=kOutput, calls=%fused_computation.13 | convolution fusion | flops 1208745984 | bytes 23592960 | tf_op jit(solution)/shard_map/cik,cjk->cij/dot_general | solution.py:376
  798.3 10.0 %bitcast_dynamic-update-slice_fusion.1 = bf16[6,64,96,128]{3,2,1,0:T(8,128)(2,1)} fusion(bf16[6,64,96,128]{3,2,1,0:T(8,128)(2,1)} %bitcast_dynamic-update-slice_fusion.2, bf16[64,96,768]{2,1,0:T(8,128)(2,1)S(1)} %constant_dynamic-update-slice_fusion, bf16[64,128,768]{2,1,0:T(8,128)(2,1)} %collective-permute-done.2), kind=kOutput, calls=%fused_computation.12 | convolution fusion | flops 1208745984 | bytes 23592960 | tf_op jit(solution)/shard_map/cik,cjk->cij/dot_general | solution.py:376
  808.3 9.8 %bitcast_dynamic-update-slice_fusion = bf16[6,64,96,128]{3,2,1,0:T(8,128)(2,1)} fusion(bf16[6,64,96,128]{3,2,1,0:T(8,128)(2,1)} %bitcast_dynamic-update-slice_fusion.1, bf16[64,96,768]{2,1,0:T(8,128)(2,1)S(1)} %constant_dynamic-update-slice_fusion, bf16[64,128,768]{2,1,0:T(8,128)(2,1)} %collective-permute-done.3), kind=kOutput, calls=%fused_computation.11 | convolution fusion | flops 1208745984 | bytes 23592960 | tf_op jit(solution)/shard_map/cik,cjk->cij/dot_general | solution.py:376
  818.1 9.1 %fusion.30 = (bf16[6,64,48,128]{3,2,1,0:T(8,128)(2,1)}, bf16[6,64,48,128]{3,2,1,0:T(8,128)(2,1)}) fusion(bf16[6,64,96,128]{3,2,1,0:T(8,128)(2,1)} %bitcast_dynamic-update-slice_fusion), kind=kLoop, calls=%fused_computation.98 | loop fusion | bytes 18874368 | tf_op jit(solution)/shard_map/slice | solution.py:383
  827.7 0.7 fusion.23.w_ref
  828.4 7.0 collective-permute-done.4.theirs_ref
  835.5 0.7 broadcast_in_dim.72.gain_ref
  836.2 57.8 %finish.1 = bf16[48,768,128]{2,1,0:T(8,128)(2,1)} custom-call(s32[1]{0:T(128)} %bitcast.10.core, bf16[6,64,48,128]{3,2,1,0:T(8,128)(2,1)} %get-tuple-element.28.mine_ref, bf16[6,64,48,128]{3,2,1,0:T(8,128)(2,1)} %collective-permute-done.4.theirs_ref, f32[48,128,768]{2,1,0:T(8,128)} %get-tuple-element.21.pair_ref, ...), custom_call_target="tpu_custom_call" | custom-call | tf_op jit(solution)/shard_map/finish/pallas_call | solution.py:224
  (87 shorter events, 11.0 us)
Async XLA Ops:
  7.2 143.0 %copy-start = (bf16[2,2560,128]{2,1,0:T(8,128)(2,1)S(1)}, bf16[2,2560,128]{2,1,0:T(8,128)(2,1)}, u32[]{:S(2)}) copy-start(bf16[2,2560,128]{2,1,0:T(8,128)(2,1)} %param.20) | copy-start | bytes 3932164
  7.2 56.2 %all-gather.3.cloned.1.call-start = ((), (), s32[]{:S(2)}) async-start(), calls=%async_computation.1 | async-start | bytes 4177920 | tf_op jit(solution)/shard_map/all_gather | solution.py:272
  11.4 137.8 %reduce-scatter.2.cloned.1.call-start = ((), (), s32[]{:S(2)}) async-start(), calls=%async_computation.2 | async-start | bytes 4177920 | tf_op jit(solution)/shard_map/reduce_scatter | solution.py:292
  75.6 6.4 copy-start.6
  75.6 8.2 copy-start.7
  75.6 10.3 %copy-start.8 = (f32[2,128]{1,0:T(2,128)S(1)}, f32[2,128]{1,0:T(2,128)}, u32[]{:S(2)}) copy-start(f32[2,128]{1,0:T(2,128)} %param.21) | copy-start | bytes 3076
  75.6 73.6 %copy-start.3 = (bf16[48,2560]{1,0:T(8,128)(2,1)S(1)}, bf16[48,2560]{1,0:T(8,128)(2,1)}, u32[]{:S(2)}) copy-start(bf16[48,2560]{1,0:T(8,128)(2,1)} %param.13) | copy-start | bytes 737284
  80.0 132.9 %all-gather.5.cloned.1.call-start = ((), (), s32[]{:S(2)}) async-start(), calls=%async_computation.3 | async-start | bytes 6684672 | tf_op jit(solution)/shard_map/all_gather | solution.py:282
  150.2 0.7 copy-start.4
  217.8 1.6 copy-start.2
  424.1 364.4 %collective-permute-start.1 = (bf16[64,128,768]{2,1,0:T(8,128)(2,1)}, bf16[64,128,768]{2,1,0:T(8,128)(2,1)}, u32[]{:S(2)}, u32[]{:S(2)}) collective-permute-start(bf16[64,128,768]{2,1,0:T(8,128)(2,1)} %get-tuple-element.18), channel_id=1, source_target_pairs={{0,1},{1,0},{2,3},{3,2},{4,5},{5,4},{6,7},{7,6},{8,9},{9,8},{10,11... | collective-permute-start | bytes 37748744 | tf_op jit(solution)/shard_map/ppermute | solution.py:361
  547.5 250.8 %collective-permute-start.2 = (bf16[64,128,768]{2,1,0:T(8,128)(2,1)}, bf16[64,128,768]{2,1,0:T(8,128)(2,1)}, u32[]{:S(2)}, u32[]{:S(2)}) collective-permute-start(bf16[64,128,768]{2,1,0:T(8,128)(2,1)} %get-tuple-element.19), channel_id=1, source_target_pairs={{0,1},{1,0},{2,3},{3,2},{4,5},{5,4},{6,7},{7,6},{8,9},{9,8},{10,11... | collective-permute-start | bytes 37748744 | tf_op jit(solution)/shard_map/ppermute | solution.py:361
  671.0 137.4 %collective-permute-start.3 = (bf16[64,128,768]{2,1,0:T(8,128)(2,1)}, bf16[64,128,768]{2,1,0:T(8,128)(2,1)}, u32[]{:S(2)}, u32[]{:S(2)}) collective-permute-start(bf16[64,128,768]{2,1,0:T(8,128)(2,1)} %get-tuple-element.20), channel_id=1, source_target_pairs={{0,1},{1,0},{2,3},{3,2},{4,5},{5,4},{6,7},{7,6},{8,9},{9,8},{10,11... | collective-permute-start | bytes 37748744 | tf_op jit(solution)/shard_map/ppermute | solution.py:361
  750.3 8.1 collective-permute-start
  818.1 9.4 %copy-start.9 = (f32[128]{0:T(128)S(1)}, f32[128]{0:T(128)}, u32[]{:S(2)}) copy-start(f32[128]{0:T(128)} %get-tuple-element.61) | copy-start | bytes 1540
  818.1 9.5 %copy-start.5 = (bf16[128,128]{1,0:T(8,128)(2,1)S(1)}, bf16[128,128]{1,0:T(8,128)(2,1)}, u32[]{:S(2)}) copy-start(bf16[128,128]{1,0:T(8,128)(2,1)} %param.23) | copy-start | bytes 98308
  827.2 8.3 collective-permute-start.4
  836.2 57.8 %copy-start.1 = (bf16[2,2560,128]{2,1,0:T(8,128)(2,1)S(1)}, bf16[2,2560,128]{2,1,0:T(8,128)(2,1)}, u32[]{:S(2)}) copy-start(bf16[2,2560,128]{2,1,0:T(8,128)(2,1)} %param.20) | copy-start | bytes 3932164
Sparse Core Ops, SparseCore 0:
  11.5 51.7 all-gather.2
  80.1 69.0 reduce-scatter.1
  151.5 61.3 all-gather.4

commit v2 on v1

--- a/solution.py
+++ b/solution.py
@@ -12,6 +12,7 @@
 BIN_ROWS = 80
 LANES = 128
 CHUNKS = 3
+PAD = 8
 VMEM_BYTES = 60 * 1024 * 1024
 
 
@@ -49,20 +50,20 @@
         top = jnp.max(scores, axis=-1, keepdims=True)
         powers = jnp.exp(scores - top)
         probs = powers / jnp.sum(powers, axis=-1, keepdims=True)
-        start = pl.multiple_of(h * rows, 8)
+        start = pl.multiple_of(h * (rows + PAD), 8)
         for n in range(blocks):
             scratch[n, pl.ds(start, rows), :] = probs[:, n * LANES : (n + 1) * LANES]
         return carry
 
-    lax.fori_loop(0, heads, one_head, 0, unroll=2)
+    lax.fori_loop(0, heads, one_head, 0, unroll=8)
 
     def one_row(j, carry):
         for n in range(blocks):
-            rows_of = scratch[n, pl.ds(j, heads, stride=rows), :]
+            rows_of = scratch[n, pl.ds(j, heads, stride=rows + PAD), :]
             out_ref[j, :, n * LANES : (n + 1) * LANES] = rows_of.astype(jnp.bfloat16)
         return carry
 
-    lax.fori_loop(0, rows, one_row, 0, unroll=2)
+    lax.fori_loop(0, rows, one_row, 0, unroll=8)
 
 
 def attention_maps(queries, keys, block):
@@ -77,7 +78,7 @@
             pl.BlockSpec((heads, width, length), lambda b: (0, 0, 0)),
         ],
         out_specs=pl.BlockSpec((block, heads, length), lambda b: (b, 0, 0)),
-        scratch_shapes=[pltpu.VMEM((length // LANES, heads * block, LANES), jnp.float32)],
+        scratch_shapes=[pltpu.VMEM((length // LANES, heads * (block + PAD), LANES), jnp.float32)],
         compiler_params=pltpu.CompilerParams(vmem_limit_bytes=VMEM_BYTES),
         cost_estimate=pl.CostEstimate(
             flops=2 * heads * rows * length * width * 4,
@@ -119,7 +120,7 @@
             )
             value = gated[:channels]
             edge = value + value * jnp.tanh(gated[channels : 2 * channels])
-            start = pl.multiple_of(j * channels, 8)
+            start = pl.multiple_of(j * (channels + PAD), 8)
             for m in range(width // LANES):
                 scratch[n * (width // LANES) + m, pl.ds(start, channels), :] = edge[
                     :, m * LANES : (m + 1) * LANES
@@ -131,17 +132,17 @@
                 )
         return carry
 
-    lax.fori_loop(0, block, one_row, 0)
+    lax.fori_loop(0, block, one_row, 0, unroll=8)
     half = channels // 2
 
     def one_channel(c, carry):
         for n in range(length // LANES):
             for side in range(2):
-                rows_of = scratch[n, pl.ds(c + side * half, block, stride=channels), :]
+                rows_of = scratch[n, pl.ds(c + side * half, block, stride=channels + PAD), :]
                 rest[side][c, :, n * LANES : (n + 1) * LANES] = rows_of.astype(jnp.bfloat16)
         return carry
 
-    lax.fori_loop(0, half, one_channel, 0, unroll=2)
+    lax.fori_loop(0, half, one_channel, 0, unroll=16)
 
 
 def edges(own, row_index, maps, mix, right, gain, weights, cols, block, skip=0, rows=None):
@@ -173,7 +174,7 @@
                 pl.BlockSpec(cols.shape, lambda b, s: (0, 0)),
             ],
             out_specs=out_specs,
-            scratch_shapes=[pltpu.VMEM((length // LANES, block * channels, LANES), jnp.float32)],
+            scratch_shapes=[pltpu.VMEM((length // LANES, block * (channels + PAD), LANES), jnp.float32)],
         ),
         compiler_params=pltpu.CompilerParams(vmem_limit_bytes=VMEM_BYTES),
         cost_estimate=pl.CostEstimate(
@@ -190,15 +191,15 @@
     for n, ref in enumerate((mine_ref, theirs_ref)):
 
         def one_channel(c, carry):
-            start = pl.multiple_of(c * block, 8)
+            start = pl.multiple_of(c * (block + PAD), 8)
             scratch[n, pl.ds(start, block), :] = ref[0, c].astype(jnp.float32)
             return carry
 
-        lax.fori_loop(0, half, one_channel, 0, unroll=4)
+        lax.fori_loop(0, half, one_channel, 0, unroll=8)
 
     def one_row(i, carry):
         products = jnp.concatenate(
-            [scratch[n, pl.ds(i, half, stride=block), :] for n in range(2)], axis=0
+            [scratch[n, pl.ds(i, half, stride=block + PAD), :] for n in range(2)], axis=0
         )
         center = jnp.mean(products, axis=0, keepdims=True)
         centered = products - center
@@ -209,7 +210,7 @@
         out_ref[i] = total.T.astype(jnp.bfloat16)
         return carry
 
-    lax.fori_loop(0, block, one_row, 0, unroll=2)
+    lax.fori_loop(0, block, one_row, 0, unroll=16)
 
 
 def finish(core, mine, theirs, pair, gate, gain, weights, block):
@@ -238,7 +239,7 @@
                 pl.BlockSpec(weights.shape, lambda b, u, s: (0, 0)),
             ],
             out_specs=pl.BlockSpec((block, width, channels), lambda b, u, s: (b, column(u, s), 0)),
-            scratch_shapes=[pltpu.VMEM((2, half * block, width), jnp.float32)],
+            scratch_shapes=[pltpu.VMEM((2, half * (block + PAD), width), jnp.float32)],
         ),
         compiler_params=pltpu.CompilerParams(vmem_limit_bytes=VMEM_BYTES),
         name="finish",
@@ -280,8 +281,6 @@
     value_rows = projected[2].astype(jnp.bfloat16)
     both = jnp.stack([queries.reshape(length, -1).T, key_rows.reshape(length, -1).T])
     gathered = lax.all_gather(both, "mp", axis=1, tiled=True)
-    all_keys = gathered[1].reshape(heads, HD, length)
-    all_queries = gathered[0].reshape(heads, HD, length).transpose(0, 2, 1)
 
     scores = jnp.einsum("qhd,khd->hqk", queries, key_rows, preferred_element_type=jnp.float32)
     attn_probs = jax.nn.softmax(scores, axis=-1).astype(jnp.bfloat16)
@@ -289,13 +288,15 @@
         "hqk,khd->qhd", attn_probs, value_rows, preferred_element_type=jnp.float32
     )
     attended = attended.astype(jnp.bfloat16).reshape(length, local_heads * HD)
-    mixed = lax.psum_scatter(
-        jnp.dot(attended, w_out, preferred_element_type=jnp.float32).astype(jnp.bfloat16),
-        "mp",
-        scatter_dimension=0,
-        tiled=True,
-    ).astype(jnp.float32)
-    hidden_out = (hidden_in.astype(jnp.float32) + mixed).astype(jnp.bfloat16)
+    partial, gathered = lax.optimization_barrier(
+        (
+            jnp.dot(attended, w_out, preferred_element_type=jnp.float32).astype(jnp.bfloat16),
+            gathered,
+        )
+    )
+    all_keys = gathered[1].reshape(heads, HD, length)
+    all_queries = gathered[0].reshape(heads, HD, length).transpose(0, 2, 1)
+    mixed = lax.psum_scatter(partial, "mp", scatter_dimension=0, tiled=True)
 
     half_rows = length // 2
     row_start = me * local_rows
@@ -308,6 +309,8 @@
         lax.dynamic_slice_in_dim(all_queries, half_start, half_rows, 1), all_keys, map_block
     )
 
+    mixed, own_maps, half_maps = lax.optimization_barrier((mixed, own_maps, half_maps))
+    hidden_out = (hidden_in.astype(jnp.float32) + mixed.astype(jnp.float32)).astype(jnp.bfloat16)
     side_terms = jnp.einsum(
         "rd,sdc->src", hidden_out, w_side, preferred_element_type=jnp.float32
     ).astype(jnp.bfloat16)

time: 901 us -> 616 us (0.68)
  Pallas kernels: 579 us -> 311 us
  waiting for transfers between devices: 155 us -> 139 us
    pallas_call x4, Pallas kernels: 432 us -> 253 us  [edges(): pl.pallas_call(functools.partial(edges_kernel, own), out_shape=out_shape,...]
    pallas_call x2, Pallas kernels: 89.1 us -> 32.8 us  [attention_maps(): pl.pallas_call(maps_kernel, out_shape=jax.ShapeDtypeStruct((rows, heads,...]
    reduce_scatter x1, waiting for transfers between devices: 62.2 us -> 25.3 us  [per_device(): mixed = lax.psum_scatter(partial, 'mp', scatter_dimension=0, tiled=True)]
    pallas_call x1, Pallas kernels: 57.8 us -> 25.6 us  [finish(): pl.pallas_call(final_kernel, out_shape=jax.ShapeDtypeStruct((rows, length...]
    all_gather x1, waiting for transfers between devices: 33.5 us -> 53.8 us  [per_device(): gathered = lax.all_gather(both, 'mp', axis=1, tiled=True)]
  transfers between devices with their start and end apart: 8 -> 8, of which waited for: 5 -> 5; matrix products, arithmetic and copies ran while one was open for 9% -> 14% of each run, Pallas kernels for 36% -> 35%
where the time goes in v2:
time: 616 us; the launch traced here: 607 us
  Pallas kernels  311 us (50%)
  waiting for transfers between devices  139 us (23%)
  matrix products  70.1 us (11%)
  local copies, waits for them, and re-layouts  40.7 us (7%)
  blocking collectives  20.6 us (3%)
  between operations  14.4 us (2%)
  other arithmetic  9.84 us (2%)
    pallas_call x4, Pallas kernels, edges(): pl.pallas_call(functools.partial(edges_kernel, own), out_shape=out_shape,...  253 us
    dot_general x6, matrix products, per_device(): jnp.einsum('cik,cjk->cij', lefts, part, preferred_element_type=jnp.float32)  59 us
    all_gather x1, waiting for transfers between devices, per_device(): gathered = lax.all_gather(both, 'mp', axis=1, tiled=True)  53.8 us
    all_gather x1, waiting for transfers between devices, per_device(): lax.all_gather(normed, 'mp', axis=0, tiled=True)  47.4 us
    pallas_call x2, Pallas kernels, attention_maps(): pl.pallas_call(maps_kernel, out_shape=jax.ShapeDtypeStruct((rows, heads,...  32.8 us
    pallas_call x1, Pallas kernels, finish(): pl.pallas_call(final_kernel, out_shape=jax.ShapeDtypeStruct((rows, length...  25.6 us
    reduce_scatter x1, waiting for transfers between devices, per_device(): mixed = lax.psum_scatter(partial, 'mp', scatter_dimension=0, tiled=True)  25.3 us
    all_gather x1, blocking collectives, per_device(): all_sides = lax.all_gather(side_terms, 'mp', axis=1, tiled=True)  20.6 us
  transfers between devices with their start and end apart: 8, of which 5 were waited for; matrix products, arithmetic and copies ran while one was open for 14% of the time, Pallas kernels for 35%

profile of v2, /device:TPU:0, one launch (start us, length us, event | category | flops | bytes accessed | tf_op | source)
XLA Modules:
  0.0 607.3 jit_solution(2910830441446107838)
XLA Ops:
  7.2 1.2 convert_reduce_fusion
  8.4 1.2 fusion.8
  9.6 1.8 fusion.10
  11.5 4.0 copy.54
  15.9 47.4 %all-gather.3.cloned.1.call-done = bf16[768,2560]{1,0:T(8,128)(2,1)} async-done(((bf16[48,2560]{1,0:T(8,128)(2,1)}), bf16[768,2560]{1,0:T(8,128)(2,1)}) %all-gather.3.cloned.1.call-update) | async-done | bytes 3932176 | tf_op jit(solution)/shard_map/all_gather | solution.py:273
  63.4 4.4 fusion.36
  68.3 0.8 pad_maximum_fusion
  69.2 1.4 fusion.35
  70.5 1.8 fusion.2
  72.4 3.1 convolution_convert_fusion
  75.5 53.8 %all-gather.5.cloned.1.call-done = bf16[2,2048,768]{2,1,0:T(8,128)(2,1)} async-done(((bf16[2,128,768]{2,1,0:T(8,128)(2,1)}), bf16[2,2048,768]{2,1,0:T(8,128)(2,1)}) %all-gather.5.cloned.1.call-update) | async-done | bytes 6291472 | tf_op jit(solution)/shard_map/all_gather | solution.py:283
  130.9 0.6 pad_maximum_fusion.3.w_ref
  132.6 5.0 fusion.31
  137.5 1.6 copy-done.2
  139.4 0.9 copy.77
  140.3 1.6 constant_dynamic-slice_fusion.4
  142.0 2.8 copy.78
  144.8 6.6 %attention_maps.2.maps_ref = bf16[48,32,768]{2,1,0:T(8,128)(2,1)} custom-call(bf16[32,48,64]{2,1,0:T(8,128)(2,1)} %bitcast.134, bf16[32,64,768]{2,1,0:T(8,128)(2,1)} %bitcast.121), custom_call_target="tpu_custom_call" | custom-call | flops 603979776 | bytes 2359296 | tf_op jit(solution)/shard_map/attention_maps/pallas_call | solution.py:72
  151.5 26.2 %attention_maps.3.maps_ref = bf16[384,32,768]{2,1,0:T(8,128)(2,1)} custom-call(bf16[32,384,64]{2,1,0:T(8,128)(2,1)} %bitcast.123, bf16[32,64,768]{2,1,0:T(8,128)(2,1)} %bitcast.122), custom_call_target="tpu_custom_call" | custom-call | flops 4831838208 | bytes 18874368 | tf_op jit(solution)/shard_map/attention_maps/pallas_call | solution.py:72
  177.7 25.3 %reduce-scatter.2.cloned.1.call-done = bf16[48,2560]{1,0:T(8,128)(2,1)} async-done(((bf16[768,2560]{1,0:T(8,128)(2,1)}), bf16[48,2560]{1,0:T(8,128)(2,1)}) %reduce-scatter.2.cloned.1.call-update) | async-done | bytes 245776 | tf_op jit(solution)/shard_map/reduce_scatter | solution.py:299
  202.9 1.0 fusion.11
  204.6 20.6 %all_gather.11 = bf16[2,768,128]{2,0,1:T(2,128)(2,1)S(1)} all-gather(bf16[2,48,128]{2,0,1:T(2,128)(2,1)S(1)} %copy.60), channel_id=1, replica_groups=mesh['groups'=2,'mp'=16] {'mp'}, dimensions={1}, use_global_device_ids=true | all-gather | bytes 417792 | tf_op jit(solution)/shard_map/all_gather | solution.py:317
  226.1 0.8 convert_bitcast_fusion.right_ref
  227.6 1.3 concatenate.51
  228.9 1.3 concatenate.53
  230.3 0.7 broadcast_in_dim.32.gain_ref
  231.0 72.1 %right_edges.3 = (bf16[64,128,768]{2,1,0:T(8,128)(2,1)}, bf16[64,128,768]{2,1,0:T(8,128)(2,1)}) custom-call(s32[128]{0:T(128)} %get-tuple-element.70.row_index, bf16[384,32,768]{2,1,0:T(8,128)(2,1)} %attention_maps.3.maps_ref, bf16[8,128,240]{2,1,0:T(8,128)(2,1)} %bitcast.140, f32[128,768]{1,0:T(8,128)} %convert_bitcast_fusion.right_ref, ...), custom_call_target="tpu_custom_call" | custom-call | flops 20132659200 | bytes 25165824 | tf_op jit(solution)/shard_map/right_edges/pallas_call | solution.py:162
  303.5 72.2 %right_edges.4 = (bf16[64,128,768]{2,1,0:T(8,128)(2,1)}, bf16[64,128,768]{2,1,0:T(8,128)(2,1)}) custom-call(s32[128]{0:T(128)} %get-tuple-element.69.row_index, bf16[384,32,768]{2,1,0:T(8,128)(2,1)} %attention_maps.3.maps_ref, bf16[8,128,240]{2,1,0:T(8,128)(2,1)} %bitcast.138, f32[128,768]{1,0:T(8,128)} %convert_bitcast_fusion.right_ref, ...), custom_call_target="tpu_custom_call" | custom-call | flops 20132659200 | bytes 25165824 | tf_op jit(solution)/shard_map/right_edges/pallas_call | solution.py:162
  375.8 1.3 concatenate.54
  377.3 72.8 %right_edges.5 = (bf16[64,128,768]{2,1,0:T(8,128)(2,1)}, bf16[64,128,768]{2,1,0:T(8,128)(2,1)}) custom-call(s32[128]{0:T(128)} %get-tuple-element.68.row_index, bf16[384,32,768]{2,1,0:T(8,128)(2,1)} %attention_maps.3.maps_ref, bf16[8,128,240]{2,1,0:T(8,128)(2,1)} %bitcast.139, f32[128,768]{1,0:T(8,128)} %convert_bitcast_fusion.right_ref, ...), custom_call_target="tpu_custom_call" | custom-call | flops 20132659200 | bytes 25165824 | tf_op jit(solution)/shard_map/right_edges/pallas_call | solution.py:162
  450.4 0.6 dynamic_slice.27.row_index
  451.1 0.6 pad_maximum_fusion.2.w_ref
  452.0 0.9 concatenate.48
  452.9 36.0 %own_edges.1 = (bf16[64,48,768]{2,1,0:T(8,128)(2,1)}, bf16[64,48,768]{2,1,0:T(8,128)(2,1)}, f32[48,128,768]{2,1,0:T(8,128)}, bf16[48,128,768]{2,1,0:T(8,128)(2,1)}) custom-call(s32[48]{0:T(128)} %dynamic_slice.27.row_index, bf16[48,32,768]{2,1,0:T(8,128)(2,1)} %attention_maps.2.maps_ref, bf16[3,128,240]{2,1,0:T(8,128)(2,1)} %bitcast.142, ...), custom_call_target="tpu_custom_call" | custom-call | flops 7549747200 | bytes 9437184 | tf_op jit(solution)/shard_map/own_edges/pallas_call | solution.py:162
  489.2 2.9 constant_dynamic-update-slice_fusion.1
  492.1 5.0 collective-permute-done
  497.1 0.7 constant_dynamic-update-slice_fusion
  497.8 9.8 %bitcast_dynamic-update-slice_fusion.5 = bf16[6,64,96,128]{3,2,1,0:T(8,128)(2,1)} fusion(bf16[64,96,768]{2,1,0:T(8,128)(2,1)S(1)} %constant_dynamic-update-slice_fusion, bf16[64,128,768]{2,1,0:T(8,128)(2,1)} %get-tuple-element.25), kind=kOutput, calls=%fused_computation.16 | convolution fusion | flops 1208745984 | bytes 23592960 | tf_op jit(solution)/shard_map/cik,cjk->cij/dot_general | solution.py:379
  507.6 9.8 %bitcast_dynamic-update-slice_fusion.4 = bf16[6,64,96,128]{3,2,1,0:T(8,128)(2,1)} fusion(bf16[6,64,96,128]{3,2,1,0:T(8,128)(2,1)} %bitcast_dynamic-update-slice_fusion.5, bf16[64,96,768]{2,1,0:T(8,128)(2,1)S(1)} %constant_dynamic-update-slice_fusion, bf16[64,128,768]{2,1,0:T(8,128)(2,1)} %get-tuple-element.26), kind=kOutput, calls=%fused_computation.15 | convolution fusion | flops 1208745984 | bytes 23592960 | tf_op jit(solution)/shard_map/cik,cjk->cij/dot_general | solution.py:379
  517.4 9.8 %bitcast_dynamic-update-slice_fusion.3 = bf16[6,64,96,128]{3,2,1,0:T(8,128)(2,1)} fusion(bf16[6,64,96,128]{3,2,1,0:T(8,128)(2,1)} %bitcast_dynamic-update-slice_fusion.4, bf16[64,96,768]{2,1,0:T(8,128)(2,1)S(1)} %constant_dynamic-update-slice_fusion, bf16[64,128,768]{2,1,0:T(8,128)(2,1)} %get-tuple-element.27), kind=kOutput, calls=%fused_computation.14 | convolution fusion | flops 1208745984 | bytes 23592960 | tf_op jit(solution)/shard_map/cik,cjk->cij/dot_general | solution.py:379
  527.3 9.8 %bitcast_dynamic-update-slice_fusion.2 = bf16[6,64,96,128]{3,2,1,0:T(8,128)(2,1)} fusion(bf16[6,64,96,128]{3,2,1,0:T(8,128)(2,1)} %bitcast_dynamic-update-slice_fusion.3, bf16[64,96,768]{2,1,0:T(8,128)(2,1)S(1)} %constant_dynamic-update-slice_fusion, bf16[64,128,768]{2,1,0:T(8,128)(2,1)} %collective-permute-done.1), kind=kOutput, calls=%fused_computation.13 | convolution fusion | flops 1208745984 | bytes 23592960 | tf_op jit(solution)/shard_map/cik,cjk->cij/dot_general | solution.py:379
  537.1 10.0 %bitcast_dynamic-update-slice_fusion.1 = bf16[6,64,96,128]{3,2,1,0:T(8,128)(2,1)} fusion(bf16[6,64,96,128]{3,2,1,0:T(8,128)(2,1)} %bitcast_dynamic-update-slice_fusion.2, bf16[64,96,768]{2,1,0:T(8,128)(2,1)S(1)} %constant_dynamic-update-slice_fusion, bf16[64,128,768]{2,1,0:T(8,128)(2,1)} %collective-permute-done.2), kind=kOutput, calls=%fused_computation.12 | convolution fusion | flops 1208745984 | bytes 23592960 | tf_op jit(solution)/shard_map/cik,cjk->cij/dot_general | solution.py:379
  547.1 9.8 %bitcast_dynamic-update-slice_fusion = bf16[6,64,96,128]{3,2,1,0:T(8,128)(2,1)} fusion(bf16[6,64,96,128]{3,2,1,0:T(8,128)(2,1)} %bitcast_dynamic-update-slice_fusion.1, bf16[64,96,768]{2,1,0:T(8,128)(2,1)S(1)} %constant_dynamic-update-slice_fusion, bf16[64,128,768]{2,1,0:T(8,128)(2,1)} %collective-permute-done.3), kind=kOutput, calls=%fused_computation.11 | convolution fusion | flops 1208745984 | bytes 23592960 | tf_op jit(solution)/shard_map/cik,cjk->cij/dot_general | solution.py:379
  556.9 9.1 %fusion.30 = (bf16[6,64,48,128]{3,2,1,0:T(8,128)(2,1)}, bf16[6,64,48,128]{3,2,1,0:T(8,128)(2,1)}) fusion(bf16[6,64,96,128]{3,2,1,0:T(8,128)(2,1)} %bitcast_dynamic-update-slice_fusion), kind=kLoop, calls=%fused_computation.98 | loop fusion | bytes 18874368 | tf_op jit(solution)/shard_map/slice | solution.py:386
  566.3 0.7 fusion.23.w_ref
  567.0 7.2 %collective-permute-done.4.theirs_ref = bf16[6,64,48,128]{3,2,1,0:T(8,128)(2,1)} collective-permute-done((bf16[6,64,48,128]{3,2,1,0:T(8,128)(2,1)}, bf16[6,64,48,128]{3,2,1,0:T(8,128)(2,1)}, u32[]{:S(2)}, u32[]{:S(2)}) %collective-permute-start.4) | collective-permute-done | bytes 4718624 | tf_op jit(solution)/shard_map/ppermute | solution.py:386
  574.2 0.7 broadcast_in_dim.72.gain_ref
  574.9 25.6 %finish.1 = bf16[48,768,128]{2,1,0:T(8,128)(2,1)} custom-call(s32[1]{0:T(128)} %bitcast.24.core, bf16[6,64,48,128]{3,2,1,0:T(8,128)(2,1)} %get-tuple-element.38.mine_ref, bf16[6,64,48,128]{3,2,1,0:T(8,128)(2,1)} %collective-permute-done.4.theirs_ref, f32[48,128,768]{2,1,0:T(8,128)} %get-tuple-element.31.pair_ref, ...), custom_call_target="tpu_custom_call" | custom-call | tf_op jit(solution)/shard_map/finish/pallas_call | solution.py:225
  (93 shorter events, 8.1 us)
Async XLA Ops:
  7.2 196.8 %copy-start = (bf16[2,2560,128]{2,1,0:T(8,128)(2,1)S(1)}, bf16[2,2560,128]{2,1,0:T(8,128)(2,1)}, u32[]{:S(2)}) copy-start(bf16[2,2560,128]{2,1,0:T(8,128)(2,1)} %param.20) | copy-start | bytes 3932164
  7.2 56.2 %all-gather.3.cloned.1.call-start = ((), (), s32[]{:S(2)}) async-start(), calls=%async_computation.1 | async-start | bytes 4177920 | tf_op jit(solution)/shard_map/all_gather | solution.py:273
  11.4 117.8 %all-gather.5.cloned.1.call-start = ((), (), s32[]{:S(2)}) async-start(), calls=%async_computation.2 | async-start | bytes 6684672 | tf_op jit(solution)/shard_map/all_gather | solution.py:283
  69.1 133.8 %reduce-scatter.2.cloned.1.call-start = ((), (), s32[]{:S(2)}) async-start(), calls=%async_computation.3 | async-start | bytes 4177920 | tf_op jit(solution)/shard_map/reduce_scatter | solution.py:299
  70.5 1.9 copy-start.5
  72.3 57.0 %copy-start.10 = (bf16[32,128]{1,0:T(8,128)(2,1)S(1)}, bf16[32,128]{1,0:T(8,128)(2,1)}, u32[]{:S(2)}) copy-start(bf16[32,128]{1,0:T(8,128)(2,1)} %param.18) | copy-start | bytes 24580
  72.3 57.3 %copy-start.7 = (f32[65,128]{1,0:T(8,128)S(1)}, f32[65,128]{1,0:T(8,128)}, u32[]{:S(2)}) copy-start(f32[65,128]{1,0:T(8,128)} %param.19) | copy-start | bytes 99844
  72.3 57.6 %copy-start.6 = (bf16[5,128,128]{2,1,0:T(8,128)(2,1)S(1)}, bf16[5,128,128]{2,1,0:T(8,128)(2,1)}, u32[]{:S(2)}) copy-start(bf16[5,128,128]{2,1,0:T(8,128)(2,1)} %param.22) | copy-start | bytes 491524
  72.4 57.7 %copy-start.9 = (s32[768]{0:T(1024)S(1)}, s32[768]{0:T(1024)}, u32[]{:S(2)}) copy-start(s32[768]{0:T(1024)} %param.17) | copy-start | bytes 9220
  72.4 59.2 %copy-start.11 = (f32[2,128]{1,0:T(2,128)S(1)}, f32[2,128]{1,0:T(2,128)}, u32[]{:S(2)}) copy-start(f32[2,128]{1,0:T(2,128)} %param.21) | copy-start | bytes 3076
  137.5 1.6 copy-start.2
  151.5 51.4 %copy-start.3 = (bf16[48,2560]{1,0:T(8,128)(2,1)S(1)}, bf16[48,2560]{1,0:T(8,128)(2,1)}, u32[]{:S(2)}) copy-start(bf16[48,2560]{1,0:T(8,128)(2,1)} %param.13) | copy-start | bytes 737284
  203.9 0.7 copy-start.4
  303.1 224.2 %collective-permute-start.1 = (bf16[64,128,768]{2,1,0:T(8,128)(2,1)}, bf16[64,128,768]{2,1,0:T(8,128)(2,1)}, u32[]{:S(2)}, u32[]{:S(2)}) collective-permute-start(bf16[64,128,768]{2,1,0:T(8,128)(2,1)} %get-tuple-element.28), channel_id=1, source_target_pairs={{0,1},{1,0},{2,3},{3,2},{4,5},{5,4},{6,7},{7,6},{8,9},{9,8},{10,11... | collective-permute-start | bytes 37748744 | tf_op jit(solution)/shard_map/ppermute | solution.py:364
  377.1 159.9 %collective-permute-start.2 = (bf16[64,128,768]{2,1,0:T(8,128)(2,1)}, bf16[64,128,768]{2,1,0:T(8,128)(2,1)}, u32[]{:S(2)}, u32[]{:S(2)}) collective-permute-start(bf16[64,128,768]{2,1,0:T(8,128)(2,1)} %get-tuple-element.29), channel_id=1, source_target_pairs={{0,1},{1,0},{2,3},{3,2},{4,5},{5,4},{6,7},{7,6},{8,9},{9,8},{10,11... | collective-permute-start | bytes 37748744 | tf_op jit(solution)/shard_map/ppermute | solution.py:364
  450.0 97.0 %collective-permute-start.3 = (bf16[64,128,768]{2,1,0:T(8,128)(2,1)}, bf16[64,128,768]{2,1,0:T(8,128)(2,1)}, u32[]{:S(2)}, u32[]{:S(2)}) collective-permute-start(bf16[64,128,768]{2,1,0:T(8,128)(2,1)} %get-tuple-element.30), channel_id=1, source_target_pairs={{0,1},{1,0},{2,3},{3,2},{4,5},{5,4},{6,7},{7,6},{8,9},{9,8},{10,11... | collective-permute-start | bytes 37748744 | tf_op jit(solution)/shard_map/ppermute | solution.py:364
  488.9 8.2 %collective-permute-start = (bf16[64,48,768]{2,1,0:T(8,128)(2,1)}, bf16[64,48,768]{2,1,0:T(8,128)(2,1)S(1)}, u32[]{:S(2)}, u32[]{:S(2)}) collective-permute-start(bf16[64,48,768]{2,1,0:T(8,128)(2,1)} %get-tuple-element.23), channel_id=1, source_target_pairs={{0,1},{1,0},{2,3},{3,2},{4,5},{5,4},{6,7},{7,6},{8,9},{9,8},{10,11... | collective-permute-start | bytes 14155784 | tf_op jit(solution)/shard_map/ppermute | solution.py:376
  556.9 9.3 %copy-start.12 = (f32[128]{0:T(128)S(1)}, f32[128]{0:T(128)}, u32[]{:S(2)}) copy-start(f32[128]{0:T(128)} %get-tuple-element.71) | copy-start | bytes 1540
  556.9 9.4 %copy-start.8 = (bf16[128,128]{1,0:T(8,128)(2,1)S(1)}, bf16[128,128]{1,0:T(8,128)(2,1)}, u32[]{:S(2)}) copy-start(bf16[128,128]{1,0:T(8,128)(2,1)} %param.23) | copy-start | bytes 98308
  566.0 8.3 %collective-permute-start.4 = (bf16[6,64,48,128]{3,2,1,0:T(8,128)(2,1)}, bf16[6,64,48,128]{3,2,1,0:T(8,128)(2,1)}, u32[]{:S(2)}, u32[]{:S(2)}) collective-permute-start(bf16[6,64,48,128]{3,2,1,0:T(8,128)(2,1)} %get-tuple-element.37), channel_id=1, source_target_pairs={{0,1},{1,0},{2,3},{3,2},{4,5},{5,4},{6,7},{7,6},{8,9},{9,8},{10,11... | collective-permute-start | bytes 14155784 | tf_op jit(solution)/shard_map/ppermute | solution.py:386
  574.9 25.6 %copy-start.1 = (bf16[2,2560,128]{2,1,0:T(8,128)(2,1)S(1)}, bf16[2,2560,128]{2,1,0:T(8,128)(2,1)}, u32[]{:S(2)}) copy-start(bf16[2,2560,128]{2,1,0:T(8,128)(2,1)} %param.20) | copy-start | bytes 3932164
Sparse Core Ops, SparseCore 0:
  11.5 51.7 all-gather.2
  69.2 60.0 all-gather.4
  133.7 69.1 reduce-scatter.1
